TPU v7x, 512 devices: a whole 4x4x16 slice. The times are simulated.
512 devices in a mesh: leaf: 128 (over z, y, core), rep: 4 (over x).
Axes of the slice: x: 4, y: 4, z: 16, core: 2. Of those that a mesh axis runs over, the one named last changes fastest.
Arguments:
- positions: float32 [3, 8192, 128], P(None, ('leaf', 'rep')), may hold values from -6 to 6
- density: float32 [3, 8192, 128], P(None, ('leaf', 'rep')), may hold values from -6 to 6
- near_offset: int32 [8192, 12], P(('leaf', 'rep')), may hold values from -2 to 2
- near_count: int32 [8192], P(('leaf', 'rep')), may hold values from 1 to 12
- inter_list: int32 [512, 189], P(('leaf', 'rep')), may hold values from 0 to 511
- operator_index: int32 [512, 189], P(('leaf', 'rep')), may hold values from 0 to 3
- lattice_index: int32 [512], P(('leaf', 'rep')), may hold values from 0 to 1
- up_weight: bfloat16 [512, 384], replicated, may hold values from -0.3125 to 0.3125
- m2l_operators: bfloat16 [4, 512, 512], replicated, may hold values from -0.0390625 to 0.0390625
- lattice_operators: bfloat16 [2, 512, 512], replicated, may hold values from -0.01171875 to 0.01171875
- down_weight: bfloat16 [384, 512], replicated, may hold values from -0.5 to 0.5
Outputs:
- velocity: float32 [3, 8192, 128], P(None, ('leaf', 'rep'))
Inputs may be any that keep to these rules, and one draw needn't show every extreme that they name: `near_offset`: leaf g's near source leaves are (g + offset) mod 8192; slots at or past near_count are unused.
All inputs are finite; a program needn't handle non-finite values.
Results may differ from a plain program's by a relative error of at most 0.02.
Values may be sent and summed in bfloat16 or wider, within the bound.
A program may use at most 64 MiB of HBM per device.

v0:
```python
import math
import jax
import jax.numpy as jnp
from jax import lax
from jax.sharding import PartitionSpec as P


def padded(shard, sides, width):
    for axis, dim in sides:
        size, length = (lax.axis_size(axis), shard.shape[dim])
        up = [(i, (i + 1) % size) for i in range(size)]
        down = [(j, i) for i, j in up]
        last = lax.slice_in_dim(shard, length - width, length, axis=dim)
        first = lax.slice_in_dim(shard, 0, width, axis=dim)
        before = lax.ppermute(last, axis, up)
        after = lax.ppermute(first, axis, down)
        shard = jnp.concatenate([before, shard, after], axis=dim)
    return shard


def stokes_tile(target, source_pos, source_force, live_slots):
    offsets_xyz = target[:, None, :, None] - source_pos[:, :, None, :]
    distance_sq = jnp.sum(offsets_xyz * offsets_xyz, axis=0) + 0.05
    inverse = lax.rsqrt(distance_sq)
    inverse_cube = inverse * inverse * inverse
    projected = jnp.sum(offsets_xyz * source_force[:, :, None, :], axis=0)
    kernel_terms = source_force[:, :, None, :] * inverse + offsets_xyz * (projected * inverse_cube)
    kernel_terms = kernel_terms * live_slots[None, :, None, None]
    return jnp.sum(kernel_terms, axis=(1, 3)) * (1.0 / (8.0 * math.pi))


def body(
    positions,
    density,
    near_offset,
    near_count,
    inter_list,
    operator_index,
    lattice_index,
    up_weight,
    m2l_operators,
    lattice_operators,
    down_weight,
):
    per_box = positions.shape[1]
    node_count = positions.shape[2]
    kind_count = m2l_operators.shape[0]
    stacked = jnp.concatenate([positions, density], axis=0)
    extended = padded(stacked.astype(jnp.bfloat16), ((("leaf", "rep"), 1),), per_box).astype(
        stacked.dtype
    )
    slot_range = jnp.arange(near_offset.shape[1], dtype=jnp.int32)

    def one_leaf(leaf_slot):
        target = positions[:, leaf_slot]
        source_slot = leaf_slot + near_offset[leaf_slot] + per_box
        sources = jnp.take(extended, source_slot, axis=1)
        live_slots = (slot_range < near_count[leaf_slot]).astype(jnp.float32)
        return stokes_tile(target, sources[:3], sources[3:], live_slots)

    near_part = lax.map(one_leaf, jnp.arange(per_box, dtype=jnp.int32))
    near_part = jnp.transpose(near_part, (1, 0, 2))
    damping = 1.0 / (1.0 + jnp.sum(positions * positions, axis=0))
    summed = jnp.sum(density * damping[None], axis=1).reshape(-1).astype(jnp.bfloat16)
    coarse = jnp.dot(up_weight, summed, preferred_element_type=jnp.float32).astype(jnp.bfloat16)
    coarse_row = coarse.reshape(1, -1)
    box_ids = inter_list[0]
    op_kinds = operator_index[0]
    kind_range = jnp.arange(kind_count, dtype=jnp.int32)
    selector = (op_kinds[None, :] == kind_range[:, None]).astype(jnp.float32)
    all_blocks = lax.all_gather(coarse_row, ("leaf", "rep"), axis=0, tiled=True)
    chosen = jnp.take(all_blocks, box_ids, axis=0).astype(jnp.float32)
    grouped_sum = jnp.dot(selector, chosen, precision=lax.Precision.HIGHEST)
    block_sum = jnp.sum(all_blocks.astype(jnp.float32), axis=0)
    block_sum = lax.psum(coarse.astype(jnp.float32), ("leaf", "rep"))
    total = block_sum.astype(jnp.bfloat16)
    grouped = grouped_sum.astype(jnp.bfloat16)
    local = jnp.einsum("tij,tj->i", m2l_operators, grouped, preferred_element_type=jnp.float32)
    local = local + jnp.dot(
        lattice_operators[lattice_index[0]], total, preferred_element_type=jnp.float32
    )
    local_bf = local.astype(jnp.bfloat16)
    far_part = jnp.dot(down_weight, local_bf, preferred_element_type=jnp.float32).reshape(
        3, node_count
    )
    return near_part + damping[None] * far_part[:, None, :]


def solution(mesh):
    in_specs = (
        P(None, ("leaf", "rep"), None),
        P(None, ("leaf", "rep"), None),
        P(("leaf", "rep"), None),
        P(("leaf", "rep")),
        P(("leaf", "rep"), None),
        P(("leaf", "rep"), None),
        P(("leaf", "rep")),
        P(),
        P(),
        P(),
        P(),
    )
    out_specs = P(None, ("leaf", "rep"), None)
    return jax.shard_map(body, mesh=mesh, in_specs=in_specs, out_specs=out_specs, check_vma=False)
```

profile of v0, /device:TPU:4, one launch (start us, length us, event | category | flops | bytes accessed | tf_op | source)
XLA Modules:
  0.0 417.0 jit_solution(9846070013614672958)
XLA Ops:
  1.8 3.1 collective-permute-start
  4.9 2.7 collective-permute-start.1
  8.9 108.3 %psum.7 = bf16[512]{0:T(512)(128)(2,1)S(1)} all-reduce(bf16[512]{0:T(512)(128)(2,1)S(1)} %convert_element_type.40), channel_id=1, replica_groups=mesh['leaf'=128,'rep'=4] {'leaf','rep'}, use_global_device_ids=true, to_apply=%region_7.8 | all-reduce | flops 512 | bytes 2048 | tf_op jit(solution)/shard_map/psum | solution.py:75
  117.8 136.1 %all-gather.1 = bf16[512,1,512]{2,1,0:T(2,128)(2,1)S(1)} all-gather(bf16[1,1,512]{2,1,0:T(2,128)(2,1)S(1)} %reshape.142), channel_id=2, replica_groups=mesh['leaf'=128,'rep'=4] {'leaf','rep'}, dimensions={0}, use_global_device_ids=true | all-gather | bytes 525312 | tf_op jit(solution)/shard_map/all_gather | solution.py:71
  257.8 158.6 %while.13 = (s32[]{:T(128)}, f32[16,3,128]{2,0,1:T(8,128)S(1)}, s32[16]{0:T(128)S(1)}, s32[16,12]{1,0:T(8,128)}, f32[6,48,128]{2,0,1:T(8,128)S(1)}, /*index=5*/f...) while((s32[]{:T(128)}, f32[16,3,128]{2,0,1:T(8,128)S(1)}, ...), condition=%wide.region_4.5_spmd.clone, body=%wide.region_0.4_spmd.clone.sunk | while | flops 6891705 | bytes 6684707 | solution.py:61
  260.5 1.4 fusion.33
  262.5 1.4 compare_and_fusion.3
  270.4 1.4 fusion.33
  272.4 1.4 compare_and_fusion.3
  280.3 1.4 fusion.33
  282.3 1.4 compare_and_fusion.3
  290.3 1.4 fusion.33
  292.2 1.4 compare_and_fusion.3
  300.2 1.4 fusion.33
  302.1 1.4 compare_and_fusion.3
  310.1 1.4 fusion.33
  312.0 1.4 compare_and_fusion.3
  320.0 1.4 fusion.33
  322.0 1.4 compare_and_fusion.3
  329.9 1.4 fusion.33
  331.9 1.4 compare_and_fusion.3
  339.8 1.4 fusion.33
  341.8 1.4 compare_and_fusion.3
  349.7 1.4 fusion.33
  351.7 1.4 compare_and_fusion.3
  359.6 1.4 fusion.33
  361.6 1.4 compare_and_fusion.3
  371.5 1.4 compare_and_fusion.3
  381.4 1.4 compare_and_fusion.3
  391.3 1.4 compare_and_fusion.3
  401.3 1.4 compare_and_fusion.3
  411.2 1.4 compare_and_fusion.3
  (314 shorter events, 93.6 us)
Async XLA Ops:
  0.0 255.4 %copy-start = (bf16[4,512,512]{2,1,0:T(8,128)(2,1)S(1)}, bf16[4,512,512]{2,1,0:T(8,128)(2,1)}, u32[]{:S(2)}) copy-start(bf16[4,512,512]{2,1,0:T(8,128)(2,1)} %param.21) | copy-start | bytes 6291460
  0.0 254.1 %copy-start.2 = (s32[1,189]{1,0:T(1,128)S(1)}, s32[1,189]{1,0:T(1,128)}, u32[]{:S(2)}) copy-start(s32[1,189]{1,0:T(1,128)} %param.17) | copy-start | bytes 2272
  1.8 255.9 %collective-permute-start = (bf16[6,16,128]{2,1,0:T(8,128)(2,1)S(1)}, bf16[6,16,128]{2,1,0:T(8,128)(2,1)S(1)}, u32[]{:S(2)}, u32[]{:S(2)}) collective-permute-start(bf16[6,16,128]{2,1,0:T(8,128)(2,1)S(1)} %pad_maximum_fusion), channel_id=1, source_target_pairs={{0,1},{1,2},{2,3},{3,4},{4,5},{5,6},{6,7},{7,8},{8,9},{9,10},{10,1... | collective-permute-start | bytes 73736 | tf_op jit(solution)/shard_map/ppermute | solution.py:15
  4.9 252.8 %collective-permute-start.1 = (bf16[6,16,128]{2,1,0:T(8,128)(2,1)S(1)}, bf16[6,16,128]{2,1,0:T(8,128)(2,1)S(1)}, u32[]{:S(2)}, u32[]{:S(2)}) collective-permute-start(bf16[6,16,128]{2,1,0:T(8,128)(2,1)S(1)} %pad_maximum_fusion), channel_id=1, source_target_pairs={{1,0},{2,1},{3,2},{4,3},{5,4},{6,5},{7,6},{8,7},{9,8},{10,9},{11,1... | collective-permute-start | bytes 73736 | tf_op jit(solution)/shard_map/ppermute | solution.py:16
  117.8 137.4 %copy-start.3 = (s32[1,189]{1,0:T(1,128)S(1)}, s32[1,189]{1,0:T(1,128)}, u32[]{:S(2)}) copy-start(s32[1,189]{1,0:T(1,128)} %param.18) | copy-start | bytes 2272
  254.1 3.2 copy-start.1
  255.2 2.6 copy-start.4
where the time goes:
time: 420 us; the launch traced here: 417 us
  blocking collectives  244 us (58%)
  other arithmetic  83.3 us (20%)
  local copies, waits for them, and re-layouts  44.2 us (11%)
  loops' own time  34.7 us (8%)
  starting transfers between devices  5.84 us (1%)
    all_gather x1, blocking collectives, body(): all_blocks = lax.all_gather(coarse_row, ('leaf', 'rep'), axis=0, tiled=True)  136 us
    psum x1, blocking collectives, body(): block_sum = lax.psum(coarse.astype(jnp.float32), ('leaf', 'rep'))  108 us
    another operation x1, loops' own time, body(): near_part = lax.map(one_leaf, jnp.arange(per_box, dtype=jnp.int32))  34.7 us
    select_n x32, other arithmetic, one_leaf(): sources = jnp.take(extended, source_slot, axis=1)  23.5 us
    and x16, other arithmetic, one_leaf(): sources = jnp.take(extended, source_slot, axis=1)  22.2 us
    dynamic_slice x32, local copies, waits for them, and re-layouts, one_leaf(): target = positions[:, leaf_slot]  11.6 us
    convert_element_type x16, other arithmetic, one_leaf(): live_slots = (slot_range < near_count[leaf_slot]).astype(jnp.float32)  11 us
    reduce_sum x16, other arithmetic, stokes_tile(): return jnp.sum(kernel_terms, axis=(1, 3)) * (1.0 / (8.0 * math.pi))  10.7 us
  transfers between devices with their start and end apart: 2, of which 0 were waited for; matrix products, arithmetic and copies ran while one was open for 1% of the time, Pallas kernels for 0%

commit v1 on v0

--- a/solution.py
+++ b/solution.py
@@ -72,7 +72,9 @@
     chosen = jnp.take(all_blocks, box_ids, axis=0).astype(jnp.float32)
     grouped_sum = jnp.dot(selector, chosen, precision=lax.Precision.HIGHEST)
     block_sum = jnp.sum(all_blocks.astype(jnp.float32), axis=0)
-    block_sum = lax.psum(coarse.astype(jnp.float32), ("leaf", "rep"))
+    block_sum = coarse.astype(jnp.float32)
+    for d in ("rep", "leaf"):
+        block_sum = lax.psum(block_sum, axis_name=d)
     total = block_sum.astype(jnp.bfloat16)
     grouped = grouped_sum.astype(jnp.bfloat16)
     local = jnp.einsum("tij,tj->i", m2l_operators, grouped, preferred_element_type=jnp.float32)

time: 420 us -> 576 us (1.37)
  the two profiles are of different devices: /device:TPU:4 before, /device:TPU:2 now
where the time goes in v1:
time: 576 us; the launch traced here: 573 us
  blocking collectives  396 us (69%)
  other arithmetic  83.3 us (14%)
  local copies, waits for them, and re-layouts  44.2 us (8%)
  loops' own time  34.7 us (6%)
  starting transfers between devices  9.74 us (2%)
    psum x2, blocking collectives, body(): block_sum = lax.psum(block_sum, axis_name=d)  263 us
    all_gather x1, blocking collectives, body(): all_blocks = lax.all_gather(coarse_row, ('leaf', 'rep'), axis=0, tiled=True)  134 us
    another operation x1, loops' own time, body(): near_part = lax.map(one_leaf, jnp.arange(per_box, dtype=jnp.int32))  34.7 us
    select_n x32, other arithmetic, one_leaf(): sources = jnp.take(extended, source_slot, axis=1)  23.5 us
    and x16, other arithmetic, one_leaf(): sources = jnp.take(extended, source_slot, axis=1)  22.2 us
    dynamic_slice x32, local copies, waits for them, and re-layouts, one_leaf(): target = positions[:, leaf_slot]  11.6 us
  transfers between devices with their start and end apart: 2, of which 0 were waited for; matrix products, arithmetic and copies ran while one was open for 1% of the time, Pallas kernels for 0%

profile of v1, /device:TPU:2, one launch (start us, length us, event | category | flops | bytes accessed | tf_op | source)
XLA Modules:
  0.0 572.9 jit_solution(17631662634200828836)
XLA Ops:
  1.8 3.4 collective-permute-start
  5.2 6.3 %collective-permute-start.1 = (bf16[6,16,128]{2,1,0:T(8,128)(2,1)S(1)}, bf16[6,16,128]{2,1,0:T(8,128)(2,1)S(1)}, u32[]{:S(2)}, u32[]{:S(2)}) collective-permute-start(bf16[6,16,128]{2,1,0:T(8,128)(2,1)S(1)} %pad_maximum_fusion), channel_id=1, source_target_pairs={{1,0},{2,1},{3,2},{4,3},{5,4},{6,5},{7,6},{8,7},{9,8},{10,9},{11,1... | collective-permute-start | bytes 73736 | tf_op jit(solution)/shard_map/ppermute | solution.py:16
  12.7 15.9 %psum.14 = f32[512]{0:T(512)S(1)} all-reduce(bf16[512]{0:T(512)(128)(2,1)S(1)} %convert_element_type.40), channel_id=1, replica_groups=mesh['leaf'=128,'rep'=4] {'rep'}, use_global_device_ids=true, to_apply=%region_7.8 | all-reduce | flops 512 | bytes 3072 | tf_op jit(solution)/shard_map/psum | solution.py:77
  29.3 246.8 %psum.15 = bf16[512]{0:T(512)(128)(2,1)S(1)} all-reduce(f32[512]{0:T(512)S(1)} %psum.14), channel_id=1, replica_groups=mesh['leaf'=128,'rep'=4] {'leaf'}, use_global_device_ids=true, to_apply=%region_8.9 | all-reduce | flops 512 | bytes 3072 | tf_op jit(solution)/shard_map/psum | solution.py:77
  276.2 133.7 %all-gather.1 = bf16[512,1,512]{2,1,0:T(2,128)(2,1)S(1)} all-gather(bf16[1,1,512]{2,1,0:T(2,128)(2,1)S(1)} %reshape.142), channel_id=2, replica_groups=mesh['leaf'=128,'rep'=4] {'leaf','rep'}, dimensions={0}, use_global_device_ids=true | all-gather | bytes 525312 | tf_op jit(solution)/shard_map/all_gather | solution.py:71
  413.7 158.6 %while.13 = (s32[]{:T(128)}, f32[16,3,128]{2,0,1:T(8,128)S(1)}, s32[16]{0:T(128)S(1)}, s32[16,12]{1,0:T(8,128)}, f32[6,48,128]{2,0,1:T(8,128)S(1)}, /*index=5*/f...) while((s32[]{:T(128)}, f32[16,3,128]{2,0,1:T(8,128)S(1)}, ...), condition=%wide.region_4.5_spmd.clone, body=%wide.region_0.4_spmd.clone.sunk | while | flops 6891705 | bytes 6684707 | solution.py:61
  416.4 1.4 fusion.33
  418.4 1.4 compare_and_fusion.3
  426.3 1.4 fusion.33
  428.3 1.4 compare_and_fusion.3
  436.3 1.4 fusion.33
  438.2 1.4 compare_and_fusion.3
  446.2 1.4 fusion.33
  448.1 1.4 compare_and_fusion.3
  456.1 1.4 fusion.33
  458.0 1.4 compare_and_fusion.3
  466.0 1.4 fusion.33
  467.9 1.4 compare_and_fusion.3
  475.9 1.4 fusion.33
  477.9 1.4 compare_and_fusion.3
  485.8 1.4 fusion.33
  487.8 1.4 compare_and_fusion.3
  495.7 1.4 fusion.33
  497.7 1.4 compare_and_fusion.3
  507.6 1.4 compare_and_fusion.3
  517.5 1.4 compare_and_fusion.3
  527.4 1.4 compare_and_fusion.3
  537.3 1.4 compare_and_fusion.3
  545.3 1.4 fusion.33
  547.3 1.4 compare_and_fusion.3
  557.2 1.4 compare_and_fusion.3
  567.1 1.4 compare_and_fusion.3
  (315 shorter events, 95.0 us)
Async XLA Ops:
  0.0 411.3 %copy-start = (bf16[4,512,512]{2,1,0:T(8,128)(2,1)S(1)}, bf16[4,512,512]{2,1,0:T(8,128)(2,1)}, u32[]{:S(2)}) copy-start(bf16[4,512,512]{2,1,0:T(8,128)(2,1)} %param.21) | copy-start | bytes 6291460
  0.0 410.0 %copy-start.2 = (s32[1,189]{1,0:T(1,128)S(1)}, s32[1,189]{1,0:T(1,128)}, u32[]{:S(2)}) copy-start(s32[1,189]{1,0:T(1,128)} %param.17) | copy-start | bytes 2272
  1.8 411.8 %collective-permute-start = (bf16[6,16,128]{2,1,0:T(8,128)(2,1)S(1)}, bf16[6,16,128]{2,1,0:T(8,128)(2,1)S(1)}, u32[]{:S(2)}, u32[]{:S(2)}) collective-permute-start(bf16[6,16,128]{2,1,0:T(8,128)(2,1)S(1)} %pad_maximum_fusion), channel_id=1, source_target_pairs={{0,1},{1,2},{2,3},{3,4},{4,5},{5,6},{6,7},{7,8},{8,9},{9,10},{10,1... | collective-permute-start | bytes 73736 | tf_op jit(solution)/shard_map/ppermute | solution.py:15
  5.2 408.4 %collective-permute-start.1 = (bf16[6,16,128]{2,1,0:T(8,128)(2,1)S(1)}, bf16[6,16,128]{2,1,0:T(8,128)(2,1)S(1)}, u32[]{:S(2)}, u32[]{:S(2)}) collective-permute-start(bf16[6,16,128]{2,1,0:T(8,128)(2,1)S(1)} %pad_maximum_fusion), channel_id=1, source_target_pairs={{1,0},{2,1},{3,2},{4,3},{5,4},{6,5},{7,6},{8,7},{9,8},{10,9},{11,1... | collective-permute-start | bytes 73736 | tf_op jit(solution)/shard_map/ppermute | solution.py:16
  276.2 134.9 %copy-start.3 = (s32[1,189]{1,0:T(1,128)S(1)}, s32[1,189]{1,0:T(1,128)}, u32[]{:S(2)}) copy-start(s32[1,189]{1,0:T(1,128)} %param.18) | copy-start | bytes 2272
  410.1 3.2 copy-start.1
  411.1 2.6 copy-start.4
